TPU v7x, 512 devices: a whole 4x8x8 slice. The times are simulated.
512 devices in a mesh: pitch: 32 (over x, z), span: 8 (over y), row: 2 (over core).
Axes of the slice: x: 4, y: 8, z: 8, core: 2. Of those that a mesh axis runs over, the one named last changes fastest.
Arguments:
- fields: float32 [3, 512, 128, 512], P(None, 'pitch', 'span', 'row'), may hold values from -6 to 6
- diffusivity: float32 [512, 128, 512], P('pitch', 'span', 'row'), may hold values from 0.01 to 0.1
- mean_flow: bfloat16 [128, 2, 512], P('span', None, 'row'), may hold values from -6 to 6
- radial_kernel: bfloat16 [128, 128], replicated
- tracer_values: float32 [10, 1048576], P(None, ('pitch', 'span', 'row')), may hold values from -6 to 6
- tracer_cells: int32 [1048576], P(('pitch', 'span', 'row')), may hold values from 0 to 65535
- tracer_dest: int32 [1048576, 1], P(('pitch', 'span', 'row')), may hold values from 0 to 31; in each aligned block of 2048 rows (0 to 2047, 2048 to 4095, ...) at most 128 rows name the same one
- interface_map: int32 [2, 512], P('row', 'pitch'), may hold values from 0 to 511, as said below
Outputs:
- advected: float32 [3, 512, 128, 512], P(None, 'pitch', 'span', 'row')
- arrived: float32 [10, 2097152], P(None, ('pitch', 'span', 'row'))
Inputs may be any that keep to these rules, and one draw needn't show every extreme that they name: `tracer_cells`: the local index of the owning cell within the block of the device that holds the tracer, i * 16 * 256 + r * 256 + a for local indices i, r, a. `tracer_dest`: at most 128 of the tracers of one device go to one pitch index. `interface_map`: for one offset o of each draw, row 0 holds (i + o) mod 512 and row 1 holds (i - o) mod 512, so the two rows are inverse permutations.
All inputs are finite; a program needn't handle non-finite values.
Results may differ from a plain program's by a relative error of at most 0.0015.
Values may be sent and summed in bfloat16 or wider, within the bound.
A program may use at most 128 MiB of HBM per device.

v0:
```python
import jax
import jax.numpy as jnp
from jax import lax
from jax.sharding import PartitionSpec as P

SUB = 2
TIME_STEP = 0.9
AXIAL_SPEED = 0.15
PITCH_SPEED = 0.15


def swapped(block, axis, apart):
    count = lax.axis_size(axis)
    route = []
    for low in range(count):
        high = low | 1 << apart
        if high != low and high < count:
            route += [(low, high), (high, low)]
    return lax.ppermute(block, axis, route)


def padded(cells, sides, width):
    for axis, dim in sides:
        count = lax.axis_size(axis)
        head = lax.slice_in_dim(cells, 0, width, axis=dim)
        tail = lax.slice_in_dim(cells, cells.shape[dim] - width, cells.shape[dim], axis=dim)
        cells = jnp.concatenate(
            [
                lax.ppermute(tail, axis, [(i, (i + 1) % count) for i in range(count)]),
                cells,
                lax.ppermute(head, axis, [((i + 1) % count, i) for i in range(count)]),
            ],
            axis=dim,
        )
    return cells


def face_flux(left_values, right_values, left_kappa, right_kappa, face_speed):
    diffusion = -0.5 * (left_kappa + right_kappa) * (right_values - left_values)
    if face_speed is None:
        return diffusion
    return (
        jnp.maximum(face_speed, 0.0) * left_values
        + jnp.minimum(face_speed, 0.0) * right_values
        + diffusion
    )


def interface_ghost(own_face, local_map):
    across = swapped(own_face, "row", 0)
    picked = lax.all_gather(across, "pitch", axis=1, tiled=True)
    return jnp.take(picked, local_map, axis=1)


def update_core(extended, speed_axial, speed_pitch, ghost_face, wall_mask, row_id):
    along_pitch = extended[:, :, 1:-1, :]
    pitch_flux = face_flux(
        along_pitch[:3, :-1],
        along_pitch[:3, 1:],
        along_pitch[3, :-1],
        along_pitch[3, 1:],
        speed_pitch,
    )
    along_radius = extended[:, 1:-1]
    radial_flux = (
        face_flux(
            along_radius[:3, :, :-1],
            along_radius[:3, :, 1:],
            along_radius[3, :, :-1],
            along_radius[3, :, 1:],
            None,
        )
        * wall_mask[:, None]
    )
    core = extended[:, 1:-1, 1:-1]
    pitch_cells = core.shape[1]
    full_stack = jnp.concatenate(
        [core, jnp.broadcast_to(speed_axial[None, None], (1, pitch_cells) + speed_axial.shape)], 0
    )
    upstream = jnp.where(row_id == 0, full_stack[..., 0], ghost_face)
    downstream = jnp.where(row_id == 0, ghost_face, full_stack[..., -1])
    line = jnp.concatenate([upstream[..., None], full_stack, downstream[..., None]], -1)
    face_speed = 0.5 * (line[4, ..., :-1] + line[4, ..., 1:])
    axial_flux = face_flux(
        line[:3, ..., :-1], line[:3, ..., 1:], line[3, ..., :-1], line[3, ..., 1:], face_speed
    )
    divergence = (
        pitch_flux[:, 1:]
        - pitch_flux[:, :-1]
        + radial_flux[:, :, 1:]
        - radial_flux[:, :, :-1]
        + axial_flux[..., 1:]
        - axial_flux[..., :-1]
    )
    return core[:3] - TIME_STEP * divergence


def advance(state, diffusivity, speed_axial, speed_pitch, local_map, wall_mask):
    pitch_cells = state.shape[1]
    stacked = jnp.concatenate([state, diffusivity[None]], 0)
    extended = padded(stacked, (("pitch", 1), ("span", 2)), 1)
    full_stack = jnp.concatenate(
        [stacked, jnp.broadcast_to(speed_axial[None, None], (1, pitch_cells) + speed_axial.shape)],
        0,
    )
    row_id = lax.axis_index("row")
    own_face = jnp.where(row_id == 0, full_stack[..., -1], full_stack[..., 0])
    ghost_face = interface_ghost(own_face, local_map)
    return update_core(extended, speed_axial, speed_pitch, ghost_face, wall_mask, row_id)


def local(
    fields,
    diffusivity,
    mean_flow,
    radial_kernel,
    tracer_values,
    tracer_cells,
    tracer_dest,
    interface_map,
):
    radial_cells = mean_flow.shape[0]
    axial_cells = mean_flow.shape[2]
    flat_width = 2 * axial_cells
    span_id = lax.axis_index("span")
    kernel_cols = lax.dynamic_slice_in_dim(radial_kernel, span_id * radial_cells, radial_cells, 1)
    flat_rows = mean_flow.reshape(radial_cells, flat_width)
    smoothed = lax.psum_scatter(
        jnp.dot(kernel_cols, flat_rows, preferred_element_type=jnp.float32),
        "span",
        scatter_dimension=0,
        tiled=True,
    )
    smoothed = smoothed.reshape(radial_cells, 2, axial_cells)
    speed_axial = AXIAL_SPEED * (1.0 + 0.5 * jnp.tanh(smoothed[:, 0]))
    speed_pitch = PITCH_SPEED * jnp.tanh(smoothed[:, 1])
    plane_size = radial_cells * axial_cells
    sample_fields = jnp.take(fields.reshape(fields.shape[0], -1), tracer_cells, axis=1)
    sample_speed = jnp.take(
        jnp.stack([speed_axial, speed_pitch]).reshape(2, plane_size),
        tracer_cells % plane_size,
        axis=1,
    )
    sampled = jnp.concatenate([sample_fields, sample_speed], 0)
    head_rows = tracer_values[:5]
    tail_rows = tracer_values[5:]
    updated = jnp.concatenate(
        [head_rows + 0.5 * (sampled - head_rows), tail_rows + 0.8 * sampled], 0
    )
    npitch = lax.axis_size("pitch")
    capacity = 2 * tracer_values.shape[1] // npitch
    targets = tracer_dest[:, 0]
    onehot = (targets[:, None] == jnp.arange(npitch, dtype=jnp.int32)[None]).astype(jnp.int32)
    slot_index = jnp.sum((jnp.cumsum(onehot, 0) - onehot) * onehot, 1)
    position = targets * capacity + slot_index
    outgoing = (
        jnp.zeros((tracer_values.shape[0], npitch * capacity), jnp.float32)
        .at[:, position]
        .set(updated)
    )
    arrived = lax.all_to_all(outgoing, "pitch", split_axis=1, concat_axis=1, tiled=True)
    face_index = span_id * radial_cells + jnp.arange(radial_cells + 1, dtype=jnp.int32)
    total_radial = radial_cells * lax.axis_size("span")
    wall_mask = ((face_index > 0) & (face_index < total_radial)).astype(jnp.float32)
    local_map = interface_map[0]
    current = fields
    for substep in range(SUB):
        current = advance(current, diffusivity, speed_axial, speed_pitch, local_map, wall_mask)
    return (current, arrived)


def solution(mesh):
    placed = (
        P(None, "pitch", "span", "row"),
        P("pitch", "span", "row"),
        P("span", None, "row"),
        P(),
        P(None, ("pitch", "span", "row")),
        P(("pitch", "span", "row")),
        P(("pitch", "span", "row"), None),
        P("row", "pitch"),
    )
    return jax.shard_map(
        local,
        mesh=mesh,
        in_specs=placed,
        out_specs=(P(None, "pitch", "span", "row"), P(None, ("pitch", "span", "row"))),
        check_vma=False,
    )
```

profile of v0, /device:TPU:24, one launch (start us, length us, event | category | flops | bytes accessed | tf_op | source)
XLA Modules:
  0.0 287.4 jit_solution(10924218289385498217)
XLA Ops:
  7.2 1.1 copy.928
  8.4 1.3 constant_dynamic-update-slice_fusion
  9.8 0.7 fusion.65
  10.5 4.3 %collective-permute-start = (f32[4,1,16,256]{3,2,1,0:T(8,128)}, f32[4,1,16,256]{3,2,1,0:T(8,128)S(1)}, u32[]{:S(2)}, u32[]{:S(2)}) collective-permute-start(f32[4,1,16,256]{3,2,1,0:T(8,128)} %get-tuple-element.57), channel_id=1, source_target_pairs={{0,16},{16,32},{32,48},{48,64},{64,80},{80,96},{96,112},{112,128},... | collective-permute-start | bytes 196616 | tf_op jit(solution)/shard_map/ppermute | solution.py:29
  14.7 10.8 %collective-permute-start.1 = (f32[4,1,16,256]{3,2,1,0:T(8,128)}, f32[4,1,16,256]{3,2,1,0:T(8,128)}, u32[]{:S(2)}, u32[]{:S(2)}) collective-permute-start(f32[4,1,16,256]{3,2,1,0:T(8,128)} %get-tuple-element.58), channel_id=1, source_target_pairs={{16,0},{32,16},{48,32},{64,48},{80,64},{96,80},{112,96},{128,112},... | collective-permute-start | bytes 196616 | tf_op jit(solution)/shard_map/ppermute | solution.py:31
  25.6 0.9 fusion.48
  27.0 0.7 compare_and_fusion.2
  27.7 16.7 %copy.818 = f32[3,16,16,256]{0,3,2,1:T(8,128)} copy(f32[3,16,16,256]{3,2,1,0:T(8,128)S(1)} %copy-done.2) | data formatting | bytes 1572864 | tf_op args[0]
  44.4 18.2 %gather_fusion = f32[2048,3]{1,0:T(8,128)} fusion(f32[3,65536]{0,1:T(8,128)} %bitcast.121, s32[2048]{0:T(1024)S(1)} %get-tuple-element.74), kind=kCustom, calls=%fused_computation.2 | custom fusion | bytes 57344 | tf_op jit(solution)/shard_map/jit(_take)/gather | solution.py:138
  62.6 2.6 select_bitcast_fusion.1
  65.2 2.2 copy.820
  67.3 9.1 %reduce-window.6 = s32[32,16,128]{2,1,0:T(8,128)S(1)} reduce-window(s32[32,16,128]{2,1,0:T(8,128)S(1)} %fusion.43, s32[]{:T(128)} %constant.30.clone.1), window={size=1x1x128 pad=0_0x0_0x127_0}, to_apply=%region_1.0 | reduce-window | flops 8323072 | bytes 524292 | tf_op jit(solution)/shard_map/reduce-window
  77.9 0.9 pad_maximum_fusion.12
  79.0 4.7 %collective-permute-start.2 = (f32[4,18,1,256]{3,0,2,1:T(4,128)S(1)}, f32[4,18,1,256]{3,0,2,1:T(4,128)S(1)}, u32[]{:S(2)}, u32[]{:S(2)}) collective-permute-start(f32[4,18,1,256]{3,0,2,1:T(4,128)S(1)} %copy.846), channel_id=1, source_target_pairs={{0,2},{2,4},{4,6},{6,8},{8,10},{10,12},{12,14},{14,0},{1,3},{3,5},... | collective-permute-start | bytes 221192 | tf_op jit(solution)/shard_map/ppermute | solution.py:29
  83.7 1.9 collective-permute-start.3
  85.7 2.2 fusion.14
  87.9 0.7 fusion.39
  88.6 0.9 copy.769
  89.6 0.7 copy_dynamic-update-slice_fusion.2
  90.3 0.9 collective-permute-done.3
  91.3 1.2 fusion.19
  92.5 0.8 reshape.138
  93.7 0.8 copy.826
  94.6 0.8 copy.827
  95.4 0.7 bitcast_select_fusion.5
  96.1 1.9 collective-permute-start.4
  98.1 0.6 copy.819
  98.8 7.6 %gather_fusion.1 = f32[2048,2]{1,0:T(8,128)} fusion(f32[2,4096]{0,1:T(8,128)S(1)} %copy.819, s32[2048]{0:T(1024)S(1)} %get-tuple-element.75), kind=kCustom, calls=%fused_computation.3 | custom fusion | bytes 40960 | tf_op jit(solution)/shard_map/jit(_take)/gather | solution.py:139
  106.4 1.6 select_bitcast_fusion
  108.4 1.3 copy.822
  109.8 6.5 %scatter_custom_fusion = f32[10,4096]{0,1:T(8,128)S(1)} fusion(s32[2048]{0:T(1024)} %bitcast.141, f32[2048,10]{1,0:T(8,128)} %copy.822, f32[]{:T(128)} %constant.45.clone.1), kind=kCustom, calls=%fused_computation.51 | custom fusion | bytes 164352 | tf_op jit(solution)/shard_map/scatter | solution.py:159
  116.2 1.3 copy.823
  117.6 5.2 %all-to-all-start = ((f32[10,32,128]{2,0,1:T(8,128)}), f32[10,32,128]{2,0,1:T(8,128)}, u32[]{:S(2)}, u32[]{:S(2)}) async-start(f32[10,32,128]{2,0,1:T(8,128)} %copy.823), calls=%async_computation.1 | async-start | bytes 524288 | tf_op jit(solution)/shard_map/all_to_all | solution.py:161
  122.8 2.5 fusion.5
  125.3 0.8 copy.782
  126.2 51.2 %all_gather.6 = f32[5,512,16]{2,1,0:T(8,128)S(1)} all-gather(f32[5,16,16]{2,1,0:T(8,128)S(1)} %copy.782), channel_id=1, replica_groups=mesh['pitch'=32,'span'=8,'row'=2] {'pitch'}, dimensions={1}, use_global_device_ids=true | all-gather | bytes 168960 | tf_op jit(solution)/shard_map/all_gather | solution.py:51
  177.3 2.2 copy.783
  179.5 2.8 gather_fusion.2
  182.4 1.5 fusion.46
  183.9 2.2 copy.786
  186.1 1.4 copy.789
  187.5 2.0 fusion.2
  189.9 0.9 copy-done.5
  190.8 0.8 fusion.23
  192.4 1.0 fusion.60
  193.4 1.9 copy.834
  195.3 0.8 copy.835
  196.2 1.9 collective-permute-start.9
  198.1 0.6 fusion.64
  198.8 2.7 collective-permute-start.5
  201.4 6.5 %collective-permute-start.6 = (f32[4,1,16,256]{3,2,1,0:T(8,128)S(1)}, f32[4,1,16,256]{3,2,1,0:T(8,128)S(1)}, u32[]{:S(2)}, u32[]{:S(2)}) collective-permute-start(f32[4,1,16,256]{3,2,1,0:T(8,128)S(1)} %get-tuple-element.54), channel_id=1, source_target_pairs={{16,0},{32,16},{48,32},{64,48},{80,64},{96,80},{112,96},{128,112},... | collective-permute-start | bytes 196616 | tf_op jit(solution)/shard_map/ppermute | solution.py:31
  208.0 47.9 %all_gather.7 = f32[5,512,16]{2,1,0:T(8,128)S(1)} all-gather(f32[5,16,16]{2,1,0:T(8,128)S(1)} %copy.807), channel_id=1, replica_groups=mesh['pitch'=32,'span'=8,'row'=2] {'pitch'}, dimensions={1}, use_global_device_ids=true | all-gather | bytes 168960 | tf_op jit(solution)/shard_map/all_gather | solution.py:51
  255.8 2.2 copy.808
  258.0 2.1 gather_fusion.3
  260.8 1.4 copy.814
  262.2 1.8 fusion.3
  264.8 4.3 %collective-permute-start.7 = (f32[4,18,1,256]{3,0,2,1:T(4,128)S(1)}, f32[4,18,1,256]{3,0,2,1:T(4,128)S(1)}, u32[]{:S(2)}, u32[]{:S(2)}) collective-permute-start(f32[4,18,1,256]{3,0,2,1:T(4,128)S(1)} %copy.851), channel_id=1, source_target_pairs={{0,2},{2,4},{4,6},{6,8},{8,10},{10,12},{12,14},{14,0},{1,3},{3,5},... | collective-permute-start | bytes 221192 | tf_op jit(solution)/shard_map/ppermute | solution.py:29
  269.0 2.1 collective-permute-start.8
  271.4 1.0 fusion.8
  272.5 0.7 copy_dynamic-update-slice_fusion
  273.2 3.3 %collective-permute-done.8 = f32[4,18,1,256]{3,0,2,1:T(4,128)S(1)} collective-permute-done((f32[4,18,1,256]{3,0,2,1:T(4,128)S(1)}, f32[4,18,1,256]{3,0,2,1:T(4,128)S(1)}, u32[]{:S(2)}, u32[]{:S(2)}) %collective-permute-start.8) | collective-permute-done | bytes 73760 | tf_op jit(solution)/shard_map/ppermute | solution.py:31
  277.4 1.3 copy.825
  278.7 1.0 copy.824
  279.7 0.9 copy.857
  (102 shorter events, 7.0 us)
Async XLA Ops:
  7.2 18.4 %copy-start = (bf16[128,128]{1,0:T(8,128)(2,1)S(1)}, bf16[128,128]{1,0:T(8,128)(2,1)}, u32[]{:S(2)}) copy-start(bf16[128,128]{1,0:T(8,128)(2,1)} %param.13) | copy-start | bytes 98308
  7.2 85.3 %reduce-scatter.2.cloned.1.call-start = ((), (), s32[]{:S(2)}) async-start(), calls=%async_computation.2 | async-start | bytes 294912 | tf_op jit(solution)/shard_map/reduce_scatter | solution.py:128
  8.3 17.2 %copy-start.12 = (bf16[16,2,256]{2,1,0:T(2,128)(2,1)S(1)}, bf16[16,2,256]{2,1,0:T(2,128)(2,1)}, u32[]{:S(2)}) copy-start(bf16[16,2,256]{2,1,0:T(2,128)(2,1)} %param.12) | copy-start | bytes 49156
  8.3 18.2 %copy-start.2 = (f32[3,16,16,256]{3,2,1,0:T(8,128)S(1)}, f32[3,16,16,256]{3,2,1,0:T(8,128)}, u32[]{:S(2)}) copy-start(f32[3,16,16,256]{3,2,1,0:T(8,128)} %param.10) | copy-start | bytes 2359300
  9.8 17.2 %copy-start.16 = (s32[1,16]{1,0:T(1,128)S(1)}, s32[1,16]{1,0:T(1,128)}, u32[]{:S(2)}) copy-start(s32[1,16]{1,0:T(1,128)} %param.17) | copy-start | bytes 196
  9.8 17.9 %copy-start.11 = (s32[2048]{0:T(1024)S(1)}, s32[2048]{0:T(1024)}, u32[]{:S(2)}) copy-start(s32[2048]{0:T(1024)} %param.15) | copy-start | bytes 24580
  10.5 67.4 %collective-permute-start = (f32[4,1,16,256]{3,2,1,0:T(8,128)}, f32[4,1,16,256]{3,2,1,0:T(8,128)S(1)}, u32[]{:S(2)}, u32[]{:S(2)}) collective-permute-start(f32[4,1,16,256]{3,2,1,0:T(8,128)} %get-tuple-element.57), channel_id=1, source_target_pairs={{0,16},{16,32},{32,48},{48,64},{64,80},{80,96},{96,112},{112,128},... | collective-permute-start | bytes 196616 | tf_op jit(solution)/shard_map/ppermute | solution.py:29
  14.7 63.1 %collective-permute-start.1 = (f32[4,1,16,256]{3,2,1,0:T(8,128)}, f32[4,1,16,256]{3,2,1,0:T(8,128)}, u32[]{:S(2)}, u32[]{:S(2)}) collective-permute-start(f32[4,1,16,256]{3,2,1,0:T(8,128)} %get-tuple-element.58), channel_id=1, source_target_pairs={{16,0},{32,16},{48,32},{64,48},{80,64},{96,80},{112,96},{128,112},... | collective-permute-start | bytes 196616 | tf_op jit(solution)/shard_map/ppermute | solution.py:31
  27.0 66.3 %copy-start.3 = (f32[3,16,16,256]{3,1,2,0:T(8,128)}, f32[3,16,16,256]{3,1,2,0:T(8,128)S(1)}, u32[]{:S(2)}) copy-start(f32[3,16,16,256]{3,1,2,0:T(8,128)S(1)} %copy.791) | copy-start | bytes 2359300
  62.6 4.7 %copy-start.10 = (s32[2048,1]{0,1:T(1,128)S(1)}, s32[2048,1]{0,1:T(1,128)}, u32[]{:S(2)}) copy-start(s32[2048,1]{0,1:T(1,128)} %param.16) | copy-start | bytes 24580
  77.9 13.4 %copy-start.13 = (f32[17]{0:T(128)}, f32[17]{0:T(128)S(1)}, u32[]{:S(2)}) copy-start(f32[17]{0:T(128)S(1)} %and_convert_fusion) | copy-start | bytes 208
  79.0 10.6 %collective-permute-start.2 = (f32[4,18,1,256]{3,0,2,1:T(4,128)S(1)}, f32[4,18,1,256]{3,0,2,1:T(4,128)S(1)}, u32[]{:S(2)}, u32[]{:S(2)}) collective-permute-start(f32[4,18,1,256]{3,0,2,1:T(4,128)S(1)} %copy.846), channel_id=1, source_target_pairs={{0,2},{2,4},{4,6},{6,8},{8,10},{10,12},{12,14},{14,0},{1,3},{3,5},... | collective-permute-start | bytes 221192 | tf_op jit(solution)/shard_map/ppermute | solution.py:29
  83.7 7.5 %collective-permute-start.3 = (f32[4,18,1,256]{3,0,2,1:T(4,128)S(1)}, f32[4,18,1,256]{3,0,2,1:T(4,128)S(1)}, u32[]{:S(2)}, u32[]{:S(2)}) collective-permute-start(f32[4,18,1,256]{3,0,2,1:T(4,128)S(1)} %copy.847), channel_id=1, source_target_pairs={{2,0},{4,2},{6,4},{8,6},{10,8},{12,10},{14,12},{0,14},{3,1},{5,3},... | collective-permute-start | bytes 221192 | tf_op jit(solution)/shard_map/ppermute | solution.py:31
  95.4 2.7 copy-start.6
  96.1 29.2 %collective-permute-start.4 = (f32[5,16,16]{2,0,1:T(8,128)}, f32[5,16,16]{2,0,1:T(8,128)}, u32[]{:S(2)}, u32[]{:S(2)}) collective-permute-start(f32[5,16,16]{2,0,1:T(8,128)} %bitcast_select_fusion.5), channel_id=1, source_target_pairs={{0,1},{1,0},{2,3},{3,2},{4,5},{5,4},{6,7},{7,6},{8,9},{9,8},{10,11... | collective-permute-start | bytes 15368 | tf_op jit(solution)/shard_map/ppermute | solution.py:19
  106.4 1.9 copy-start.8
  106.4 1.9 copy-start.9
  117.6 161.1 %all-to-all-start = ((f32[10,32,128]{2,0,1:T(8,128)}), f32[10,32,128]{2,0,1:T(8,128)}, u32[]{:S(2)}, u32[]{:S(2)}) async-start(f32[10,32,128]{2,0,1:T(8,128)} %copy.823), calls=%async_computation.1 | async-start | bytes 524288 | tf_op jit(solution)/shard_map/all_to_all | solution.py:161
  177.3 5.0 %copy-start.7 = (f32[5,16,16,1]{2,0,1,3:T(8,128)S(1)}, f32[5,16,16,1]{2,0,1,3:T(8,128)}, u32[]{:S(2)}) copy-start(f32[5,16,16,1]{2,0,1,3:T(8,128)} %copy-done.6) | copy-start | bytes 15364
  177.3 5.0 %copy-start.15 = (pred[16]{0:T(512)(128)(4,1)S(1)}, pred[16]{0:T(512)(128)(4,1)}, u32[]{:S(2)}) copy-start(pred[16]{0:T(512)(128)(4,1)} %compare_and_fusion.2) | copy-start | bytes 52
  179.5 8.0 %copy-start.4 = (f32[3,16,16,256]{3,1,2,0:T(8,128)S(1)}, f32[3,16,16,256]{3,1,2,0:T(8,128)}, u32[]{:S(2)}) copy-start(f32[3,16,16,256]{3,1,2,0:T(8,128)} %copy-done.3) | copy-start | bytes 2359300
  189.6 1.2 copy-start.5
  196.2 11.7 %collective-permute-start.9 = (f32[5,16,16]{2,0,1:T(8,128)S(1)}, f32[5,16,16]{2,0,1:T(8,128)S(1)}, u32[]{:S(2)}, u32[]{:S(2)}) collective-permute-start(f32[5,16,16]{2,0,1:T(8,128)S(1)} %bitcast_select_fusion.2), channel_id=1, source_target_pairs={{0,1},{1,0},{2,3},{3,2},{4,5},{5,4},{6,7},{7,6},{8,9},{9,8},{10,11... | collective-permute-start | bytes 15368 | tf_op jit(solution)/shard_map/ppermute | solution.py:19
  198.8 65.5 %collective-permute-start.5 = (f32[4,1,16,256]{3,2,1,0:T(8,128)}, f32[4,1,16,256]{3,2,1,0:T(8,128)S(1)}, u32[]{:S(2)}, u32[]{:S(2)}) collective-permute-start(f32[4,1,16,256]{3,2,1,0:T(8,128)} %get-tuple-element.53), channel_id=1, source_target_pairs={{0,16},{16,32},{32,48},{48,64},{64,80},{80,96},{96,112},{112,128},... | collective-permute-start | bytes 196616 | tf_op jit(solution)/shard_map/ppermute | solution.py:29
  201.4 62.9 %collective-permute-start.6 = (f32[4,1,16,256]{3,2,1,0:T(8,128)S(1)}, f32[4,1,16,256]{3,2,1,0:T(8,128)S(1)}, u32[]{:S(2)}, u32[]{:S(2)}) collective-permute-start(f32[4,1,16,256]{3,2,1,0:T(8,128)S(1)} %get-tuple-element.54), channel_id=1, source_target_pairs={{16,0},{32,16},{48,32},{64,48},{80,64},{96,80},{112,96},{128,112},... | collective-permute-start | bytes 196616 | tf_op jit(solution)/shard_map/ppermute | solution.py:31
  264.8 7.7 %collective-permute-start.7 = (f32[4,18,1,256]{3,0,2,1:T(4,128)S(1)}, f32[4,18,1,256]{3,0,2,1:T(4,128)S(1)}, u32[]{:S(2)}, u32[]{:S(2)}) collective-permute-start(f32[4,18,1,256]{3,0,2,1:T(4,128)S(1)} %copy.851), channel_id=1, source_target_pairs={{0,2},{2,4},{4,6},{6,8},{8,10},{10,12},{12,14},{14,0},{1,3},{3,5},... | collective-permute-start | bytes 221192 | tf_op jit(solution)/shard_map/ppermute | solution.py:29
  269.0 7.5 %collective-permute-start.8 = (f32[4,18,1,256]{3,0,2,1:T(4,128)S(1)}, f32[4,18,1,256]{3,0,2,1:T(4,128)S(1)}, u32[]{:S(2)}, u32[]{:S(2)}) collective-permute-start(f32[4,18,1,256]{3,0,2,1:T(4,128)S(1)} %copy.852), channel_id=1, source_target_pairs={{2,0},{4,2},{6,4},{8,6},{10,8},{12,10},{14,12},{0,14},{3,1},{5,3},... | collective-permute-start | bytes 221192 | tf_op jit(solution)/shard_map/ppermute | solution.py:31
  272.4 4.2 %copy-start.14 = (f32[17]{0:T(128)S(1)}, f32[17]{0:T(128)}, u32[]{:S(2)}) copy-start(f32[17]{0:T(128)} %copy-done.13) | copy-start | bytes 208
  276.9 3.7 %copy-start.1 = (bf16[128,128]{1,0:T(8,128)(2,1)S(1)}, bf16[128,128]{1,0:T(8,128)(2,1)}, u32[]{:S(2)}) copy-start(bf16[128,128]{1,0:T(8,128)(2,1)} %param.13) | copy-start | bytes 98308
Sparse Core Ops, SparseCore 0:
  26.7 35.2 reduce-scatter.1
where the time goes:
time: 289 us; the launch traced here: 287 us
  blocking collectives  99 us (34%)
  local copies, waits for them, and re-layouts  89.4 us (31%)
  starting transfers between devices  46.3 us (16%)
  other arithmetic  32.7 us (11%)
  between operations  14.8 us (5%)
  waiting for transfers between devices  4.27 us (1%)
    all_gather x2, blocking collectives, interface_ghost(): picked = lax.all_gather(across, 'pitch', axis=1, tiled=True)  99 us
    unnamed x53, local copies, waits for them, and re-layouts  24.7 us
    ppermute x4, starting transfers between devices, padded(): lax.ppermute(head, axis, [((i + 1) % count, i) for i in range(count)])  21.3 us
    gather x1, local copies, waits for them, and re-layouts, local(): jnp.take(fields.reshape(fields.shape[0], -1), tracer_cells, axis=1)  18.2 us
    ppermute x4, starting transfers between devices, padded(): lax.ppermute(tail, axis, [(i, (i + 1) % count) for i in range(count)])  15.9 us
    another operation x3, other arithmetic  9.41 us
    gather x1, local copies, waits for them, and re-layouts, local(): jnp.take(jnp.stack([speed_axial, speed_pitch]).reshape(2, plane_size), tr...  7.6 us
    scatter x1, local copies, waits for them, and re-layouts, local(): outgoing = jnp.zeros((tracer_values.shape[0], npitch * capacity), jnp.flo...  6.46 us
  transfers between devices with their start and end apart: 12, of which 2 were waited for; matrix products, arithmetic and copies ran while one was open for 39% of the time, Pallas kernels for 0%

commit v1 on v0

--- a/solution.py
+++ b/solution.py
@@ -48,7 +48,8 @@
 
 def interface_ghost(own_face, local_map):
     across = swapped(own_face, "row", 0)
-    picked = lax.all_gather(across, "pitch", axis=1, tiled=True)
+    stack = jnp.stack([across] * lax.axis_size("pitch"))
+    picked = jnp.concatenate(lax.all_to_all(stack, "pitch", 0, 0), axis=1)
     return jnp.take(picked, local_map, axis=1)
 
 

time: 289 us -> 241 us (0.83)
  the two profiles are of different devices: /device:TPU:24 before, /device:TPU:30 now
where the time goes in v1:
time: 241 us; the launch traced here: 239 us
  local copies, waits for them, and re-layouts  113 us (47%)
  starting transfers between devices  59 us (24%)
  other arithmetic  40.4 us (17%)
  between operations  14.8 us (6%)
  waiting for transfers between devices  10.6 us (4%)
    unnamed x61, local copies, waits for them, and re-layouts  37.6 us
    gather x1, local copies, waits for them, and re-layouts, local(): jnp.take(fields.reshape(fields.shape[0], -1), tracer_cells, axis=1)  18.2 us
    ppermute x4, starting transfers between devices, padded(): lax.ppermute(head, axis, [((i + 1) % count, i) for i in range(count)])  17.5 us
    ppermute x4, starting transfers between devices, padded(): lax.ppermute(tail, axis, [(i, (i + 1) % count) for i in range(count)])  17.2 us
    all_to_all x2, starting transfers between devices, interface_ghost(): picked = jnp.concatenate(lax.all_to_all(stack, 'pitch', 0, 0), axis=1)  13.1 us
    reshape x4, local copies, waits for them, and re-layouts, interface_ghost(): picked = jnp.concatenate(lax.all_to_all(stack, 'pitch', 0, 0), axis=1)  10.5 us
    another operation x3, other arithmetic  9.41 us
    gather x1, local copies, waits for them, and re-layouts, local(): jnp.take(jnp.stack([speed_axial, speed_pitch]).reshape(2, plane_size), tr...  9.14 us
  transfers between devices with their start and end apart: 14, of which 4 were waited for; matrix products, arithmetic and copies ran while one was open for 44% of the time, Pallas kernels for 0%

profile of v1, /device:TPU:30, one launch (start us, length us, event | category | flops | bytes accessed | tf_op | source)
XLA Modules:
  0.0 239.0 jit_solution(7663790292442162014)
XLA Ops:
  7.2 1.1 copy.952
  8.4 1.3 constant_dynamic-update-slice_fusion
  10.5 4.3 %collective-permute-start = (f32[4,1,16,256]{3,2,1,0:T(8,128)}, f32[4,1,16,256]{3,2,1,0:T(8,128)S(1)}, u32[]{:S(2)}, u32[]{:S(2)}) collective-permute-start(f32[4,1,16,256]{3,2,1,0:T(8,128)} %get-tuple-element.57), channel_id=1, source_target_pairs={{0,16},{16,32},{32,48},{48,64},{64,80},{80,96},{96,112},{112,128},... | collective-permute-start | bytes 196616 | tf_op jit(solution)/shard_map/ppermute | solution.py:29
  14.7 8.9 %collective-permute-start.1 = (f32[4,1,16,256]{3,2,1,0:T(8,128)}, f32[4,1,16,256]{3,2,1,0:T(8,128)}, u32[]{:S(2)}, u32[]{:S(2)}) collective-permute-start(f32[4,1,16,256]{3,2,1,0:T(8,128)} %get-tuple-element.58), channel_id=1, source_target_pairs={{16,0},{32,16},{48,32},{64,48},{80,64},{96,80},{112,96},{128,112},... | collective-permute-start | bytes 196616 | tf_op jit(solution)/shard_map/ppermute | solution.py:31
  23.6 0.9 fusion.48
  26.9 16.6 %copy.838 = f32[3,16,16,256]{0,3,2,1:T(8,128)} copy(f32[3,16,16,256]{3,2,1,0:T(8,128)S(1)} %copy-done.2) | data formatting | bytes 1572864 | tf_op args[0]
  44.1 18.2 %gather_fusion = f32[2048,3]{1,0:T(8,128)} fusion(f32[3,65536]{0,1:T(8,128)} %bitcast.135, s32[2048]{0:T(1024)S(1)} %get-tuple-element.74), kind=kCustom, calls=%fused_computation.2 | custom fusion | bytes 57344 | tf_op jit(solution)/shard_map/jit(_take)/gather | solution.py:139
  62.3 2.6 %select_bitcast_fusion.1 = f32[3,2048]{0,1:T(8,128)} fusion(f32[2048,3]{1,0:T(8,128)} %gather_fusion, pred[2048]{0:T(1024)(128)(4,1)S(1)} %get-tuple-element.72), kind=kLoop, calls=%fused_computation.50 | loop fusion | flops 6144 | bytes 51200 | tf_op jit(solution)/shard_map/jit(_take)/select_n | solution.py:139
  64.9 1.6 copy.840
  66.4 9.1 %reduce-window.6 = s32[32,16,128]{2,1,0:T(8,128)S(1)} reduce-window(s32[32,16,128]{2,1,0:T(8,128)S(1)} %fusion.43, s32[]{:T(128)} %constant.30.clone.1), window={size=1x1x128 pad=0_0x0_0x127_0}, to_apply=%region_1.0 | reduce-window | flops 8323072 | bytes 524292 | tf_op jit(solution)/shard_map/reduce-window
  77.6 0.9 pad_maximum_fusion.12
  78.6 4.7 %collective-permute-start.2 = (f32[4,18,1,256]{3,0,2,1:T(4,128)S(1)}, f32[4,18,1,256]{3,0,2,1:T(4,128)S(1)}, u32[]{:S(2)}, u32[]{:S(2)}) collective-permute-start(f32[4,18,1,256]{3,0,2,1:T(4,128)S(1)} %copy.870), channel_id=1, source_target_pairs={{0,2},{2,4},{4,6},{6,8},{8,10},{10,12},{12,14},{14,0},{1,3},{3,5},... | collective-permute-start | bytes 221192 | tf_op jit(solution)/shard_map/ppermute | solution.py:29
  83.4 1.9 collective-permute-start.3
  85.3 2.2 fusion.14
  88.3 1.0 copy.787
  91.2 0.9 copy-done.6
  93.2 1.0 fusion.61
  94.2 1.9 copy.846
  97.6 1.9 collective-permute-start.4
  99.6 2.0 copy.839
  101.7 9.1 %gather_fusion.1 = f32[2048,2]{1,0:T(8,128)} fusion(f32[2,4096]{0,1:T(8,128)} %copy.839, s32[2048]{0:T(1024)S(1)} %copy-done.12), kind=kCustom, calls=%fused_computation.3 | custom fusion | bytes 40960 | tf_op jit(solution)/shard_map/jit(_take)/gather | solution.py:140
  110.8 1.6 select_bitcast_fusion
  112.4 0.9 copy.841
  113.3 0.9 multiply_add_fusion.3
  114.9 1.3 copy.842
  116.2 7.2 %scatter_custom_fusion = f32[10,4096]{0,1:T(8,128)} fusion(s32[2048]{0:T(1024)} %bitcast.157, f32[2048,10]{1,0:T(8,128)S(1)} %copy.842, f32[]{:T(128)} %constant.45.clone.1), kind=kCustom, calls=%fused_computation.51 | custom fusion | bytes 164352 | tf_op jit(solution)/shard_map/scatter | solution.py:160
  123.4 2.9 %copy.843 = f32[10,32,128]{2,0,1:T(8,128)} copy(f32[10,32,128]{0,2,1:T(8,128)} %bitcast.142) | data formatting | bytes 327680 | tf_op jit(solution)/shard_map/all_to_all | solution.py:162
  126.3 7.4 %all-to-all-start.2 = ((f32[10,32,128]{2,0,1:T(8,128)}), f32[10,32,128]{2,0,1:T(8,128)}, u32[]{:S(2)}, u32[]{:S(2)}) async-start(f32[10,32,128]{2,0,1:T(8,128)} %copy.843), calls=%async_computation.3 | async-start | bytes 524288 | tf_op jit(solution)/shard_map/all_to_all | solution.py:162
  133.7 2.9 %fusion.19 = f32[3,16,17,256]{3,1,2,0:T(8,128)} fusion(f32[4,18,17,256]{3,1,2,0:T(8,128)} %copy-done.8, f32[4,18,17,256]{3,1,2,0:T(8,128)} %copy-done.6, f32[17]{0:T(128)S(1)} %copy-done.16, f32[16,17,256]{2,0,1:T(8,128)S(1)} %fusion.36), kind=kLoop, calls=%fused_computation.62 | loop fusion | flops 626688 | bytes 2785348 | tf_op jit(solution)/shard_map/mul | solution.py:67
  137.5 1.2 broadcast_bitcast_fusion.1
  138.6 2.5 %reshape.211 = f32[32,1,1280]{2,1,0:T(1,128)} reshape(f32[32,5,16,16]{3,2,1,0:T(8,128)} %broadcast_bitcast_fusion.1) | data formatting | bytes 327680
  141.1 4.0 %all-to-all-done.2 = f32[10,32,128]{2,0,1:T(8,128)} async-done(((f32[10,32,128]{2,0,1:T(8,128)}), f32[10,32,128]{2,0,1:T(8,128)}, u32[]{:S(2)}, u32[]{:S(2)}) %all-to-all-start.2) | async-done | bytes 163872 | tf_op jit(solution)/shard_map/all_to_all | solution.py:162
  145.1 6.2 %all-to-all-start = ((f32[32,1,1280]{2,1,0:T(1,128)}), f32[32,1,1280]{2,1,0:T(1,128)S(1)}, u32[]{:S(2)}, u32[]{:S(2)}) async-start(f32[32,1,1280]{2,1,0:T(1,128)} %reshape.211), calls=%async_computation.1 | async-start | bytes 327680 | tf_op jit(solution)/shard_map/all_to_all | solution.py:52
  151.3 3.3 %fusion.5 = f32[3,17,16,256]{3,1,2,0:T(8,128)} fusion(f32[3,17,16,256]{3,2,1,0:T(8,128)} %get-tuple-element.56, f32[3,17,16,256]{3,2,1,0:T(8,128)S(1)} %copy-done.7, f32[17,16,256]{2,0,1:T(8,128)} %copy.787, f32[16,256]{1,0:T(8,128)S(1)} %get-tuple-element.70, f32[16,256]{1,0:T(8,128)S(1)} %get-tuple-element.71), kind=kLoop, calls=%fused_computation.32 | loop fusion | flops 1253376 | bytes 2818048 | tf_op jit(solution)/shard_map/add | solution.py:43
  154.5 1.0 copy.844
  156.4 3.4 %all-to-all-done = f32[32,1,1280]{2,1,0:T(1,128)S(1)} async-done(((f32[32,1,1280]{2,1,0:T(1,128)}), f32[32,1,1280]{2,1,0:T(1,128)S(1)}, u32[]{:S(2)}, u32[]{:S(2)}) %all-to-all-start) | async-done | bytes 163872 | tf_op jit(solution)/shard_map/all_to_all | solution.py:52
  160.4 1.1 reduce
  161.5 1.5 reshape.212
  162.9 2.5 %bitcast_bitcast_fusion.2 = f32[5,32,16,16]{2,3,0,1:T(8,128)} fusion(f32[32,5,16,16]{3,2,1,0:T(8,128)} %reshape.212), kind=kLoop, calls=%fused_computation.176 | loop fusion | bytes 327680 | tf_op jit(solution)/shard_map/reshape | solution.py:52
  165.4 2.8 %copy.849 = f32[5,32,16,16]{3,0,2,1:T(8,128)} copy(f32[5,32,16,16]{2,3,0,1:T(8,128)} %bitcast_bitcast_fusion.2) | data formatting | bytes 327680 | tf_op jit(solution)/shard_map/reshape | solution.py:52
  168.2 2.3 gather_fusion.2
  171.2 1.4 copy.808
  172.5 1.8 fusion.2
  177.5 1.0 fusion.60
  178.6 1.9 copy.855
  181.3 1.9 collective-permute-start.9
  183.3 3.4 %collective-permute-start.5 = (f32[4,1,16,256]{3,2,1,0:T(8,128)S(1)}, f32[4,1,16,256]{3,2,1,0:T(8,128)S(1)}, u32[]{:S(2)}, u32[]{:S(2)}) collective-permute-start(f32[4,1,16,256]{3,2,1,0:T(8,128)S(1)} %get-tuple-element.53), channel_id=1, source_target_pairs={{0,16},{16,32},{32,48},{48,64},{64,80},{80,96},{96,112},{112,128},... | collective-permute-start | bytes 196616 | tf_op jit(solution)/shard_map/ppermute | solution.py:29
  186.7 4.6 %collective-permute-start.6 = (f32[4,1,16,256]{3,2,1,0:T(8,128)S(1)}, f32[4,1,16,256]{3,2,1,0:T(8,128)S(1)}, u32[]{:S(2)}, u32[]{:S(2)}) collective-permute-start(f32[4,1,16,256]{3,2,1,0:T(8,128)S(1)} %get-tuple-element.54), channel_id=1, source_target_pairs={{16,0},{32,16},{48,32},{64,48},{80,64},{96,80},{112,96},{128,112},... | collective-permute-start | bytes 196616 | tf_op jit(solution)/shard_map/ppermute | solution.py:31
  191.4 1.2 broadcast_bitcast_fusion
  192.5 2.5 %reshape.213 = f32[32,1,1280]{2,1,0:T(1,128)} reshape(f32[32,5,16,16]{3,2,1,0:T(8,128)} %broadcast_bitcast_fusion) | data formatting | bytes 327680
  195.0 7.0 %all-to-all-start.1 = ((f32[32,1,1280]{2,1,0:T(1,128)}), f32[32,1,1280]{2,1,0:T(1,128)S(1)}, u32[]{:S(2)}, u32[]{:S(2)}) async-start(f32[32,1,1280]{2,1,0:T(1,128)} %reshape.213), calls=%async_computation.2 | async-start | bytes 327680 | tf_op jit(solution)/shard_map/all_to_all | solution.py:52
  202.4 4.8 %collective-permute-start.7 = (f32[4,18,1,256]{3,0,2,1:T(4,128)S(1)}, f32[4,18,1,256]{3,0,2,1:T(4,128)S(1)}, u32[]{:S(2)}, u32[]{:S(2)}) collective-permute-start(f32[4,18,1,256]{3,0,2,1:T(4,128)S(1)} %copy.875), channel_id=1, source_target_pairs={{0,2},{2,4},{4,6},{6,8},{8,10},{10,12},{12,14},{14,0},{1,3},{3,5},... | collective-permute-start | bytes 221192 | tf_op jit(solution)/shard_map/ppermute | solution.py:29
  207.2 2.1 collective-permute-start.8
  209.6 2.0 fusion.8
  212.4 2.3 collective-permute-done.8
  215.1 1.1 reduce.1
  216.1 1.5 reshape.214
  217.6 2.5 %bitcast_bitcast_fusion.1 = f32[5,32,16,16]{2,3,0,1:T(8,128)} fusion(f32[32,5,16,16]{3,2,1,0:T(8,128)} %reshape.214), kind=kLoop, calls=%fused_computation.175 | loop fusion | bytes 327680 | tf_op jit(solution)/shard_map/reshape | solution.py:52
  220.1 2.8 %copy.858 = f32[5,32,16,16]{3,0,2,1:T(8,128)} copy(f32[5,32,16,16]{2,3,0,1:T(8,128)} %bitcast_bitcast_fusion.1) | data formatting | bytes 327680 | tf_op jit(solution)/shard_map/reshape | solution.py:52
  222.9 2.3 gather_fusion.3
  225.8 1.4 copy.834
  227.2 1.8 fusion.3
  229.3 1.0 copy-done.4
  230.9 1.3 copy.845
  (117 shorter events, 22.2 us)
Async XLA Ops:
  7.2 16.5 %copy-start = (bf16[128,128]{1,0:T(8,128)(2,1)S(1)}, bf16[128,128]{1,0:T(8,128)(2,1)}, u32[]{:S(2)}) copy-start(bf16[128,128]{1,0:T(8,128)(2,1)} %param.13) | copy-start | bytes 98308
  7.2 85.0 %reduce-scatter.2.cloned.1.call-start = ((), (), s32[]{:S(2)}) async-start(), calls=%async_computation.4 | async-start | bytes 294912 | tf_op jit(solution)/shard_map/reduce_scatter | solution.py:129
  8.3 15.3 %copy-start.14 = (bf16[16,2,256]{2,1,0:T(2,128)(2,1)S(1)}, bf16[16,2,256]{2,1,0:T(2,128)(2,1)}, u32[]{:S(2)}) copy-start(bf16[16,2,256]{2,1,0:T(2,128)(2,1)} %param.12) | copy-start | bytes 49156
  8.3 16.3 %copy-start.2 = (f32[3,16,16,256]{3,2,1,0:T(8,128)S(1)}, f32[3,16,16,256]{3,2,1,0:T(8,128)}, u32[]{:S(2)}) copy-start(f32[3,16,16,256]{3,2,1,0:T(8,128)} %param.10) | copy-start | bytes 2359300
  9.8 15.3 %copy-start.17 = (s32[1,16]{1,0:T(1,128)S(1)}, s32[1,16]{1,0:T(1,128)}, u32[]{:S(2)}) copy-start(s32[1,16]{1,0:T(1,128)} %param.17) | copy-start | bytes 196
  9.8 15.9 %copy-start.13 = (s32[2048]{0:T(1024)S(1)}, s32[2048]{0:T(1024)}, u32[]{:S(2)}) copy-start(s32[2048]{0:T(1024)} %param.15) | copy-start | bytes 24580
  10.5 67.1 %collective-permute-start = (f32[4,1,16,256]{3,2,1,0:T(8,128)}, f32[4,1,16,256]{3,2,1,0:T(8,128)S(1)}, u32[]{:S(2)}, u32[]{:S(2)}) collective-permute-start(f32[4,1,16,256]{3,2,1,0:T(8,128)} %get-tuple-element.57), channel_id=1, source_target_pairs={{0,16},{16,32},{32,48},{48,64},{64,80},{80,96},{96,112},{112,128},... | collective-permute-start | bytes 196616 | tf_op jit(solution)/shard_map/ppermute | solution.py:29
  14.7 62.8 %collective-permute-start.1 = (f32[4,1,16,256]{3,2,1,0:T(8,128)}, f32[4,1,16,256]{3,2,1,0:T(8,128)}, u32[]{:S(2)}, u32[]{:S(2)}) collective-permute-start(f32[4,1,16,256]{3,2,1,0:T(8,128)} %get-tuple-element.58), channel_id=1, source_target_pairs={{16,0},{32,16},{48,32},{64,48},{80,64},{96,80},{112,96},{128,112},... | collective-permute-start | bytes 196616 | tf_op jit(solution)/shard_map/ppermute | solution.py:31
  62.3 4.1 %copy-start.11 = (s32[2048,1]{0,1:T(1,128)S(1)}, s32[2048,1]{0,1:T(1,128)}, u32[]{:S(2)}) copy-start(s32[2048,1]{0,1:T(1,128)} %param.16) | copy-start | bytes 24580
  78.6 10.6 %collective-permute-start.2 = (f32[4,18,1,256]{3,0,2,1:T(4,128)S(1)}, f32[4,18,1,256]{3,0,2,1:T(4,128)S(1)}, u32[]{:S(2)}, u32[]{:S(2)}) collective-permute-start(f32[4,18,1,256]{3,0,2,1:T(4,128)S(1)} %copy.870), channel_id=1, source_target_pairs={{0,2},{2,4},{4,6},{6,8},{8,10},{10,12},{12,14},{14,0},{1,3},{3,5},... | collective-permute-start | bytes 221192 | tf_op jit(solution)/shard_map/ppermute | solution.py:29
  83.4 7.5 %collective-permute-start.3 = (f32[4,18,1,256]{3,0,2,1:T(4,128)S(1)}, f32[4,18,1,256]{3,0,2,1:T(4,128)S(1)}, u32[]{:S(2)}, u32[]{:S(2)}) collective-permute-start(f32[4,18,1,256]{3,0,2,1:T(4,128)S(1)} %copy.871), channel_id=1, source_target_pairs={{2,0},{4,2},{6,4},{8,6},{10,8},{12,10},{14,12},{0,14},{3,1},{5,3},... | collective-permute-start | bytes 221192 | tf_op jit(solution)/shard_map/ppermute | solution.py:31
  90.0 1.2 copy-start.8
  90.9 1.2 copy-start.6
  97.0 13.8 %copy-start.9 = (f32[5,16,16,1]{2,0,1,3:T(8,128)}, f32[5,16,16,1]{2,0,1,3:T(8,128)S(1)}, u32[]{:S(2)}) copy-start(f32[5,16,16,1]{2,0,1,3:T(8,128)S(1)} %copy.847) | copy-start | bytes 15364
  97.0 4.7 %copy-start.12 = (s32[2048]{0:T(1024)S(1)}, s32[2048]{0:T(1024)}, u32[]{:S(2)}) copy-start(s32[2048]{0:T(1024)} %get-tuple-element.75) | copy-start | bytes 24580
  97.6 38.9 %collective-permute-start.4 = (f32[5,16,16]{2,0,1:T(8,128)}, f32[5,16,16]{2,0,1:T(8,128)}, u32[]{:S(2)}, u32[]{:S(2)}) collective-permute-start(f32[5,16,16]{2,0,1:T(8,128)} %bitcast_select_fusion.5), channel_id=1, source_target_pairs={{0,1},{1,0},{2,3},{3,2},{4,5},{5,4},{6,7},{7,6},{8,9},{9,8},{10,11... | collective-permute-start | bytes 15368 | tf_op jit(solution)/shard_map/ppermute | solution.py:19
  123.4 10.3 %copy-start.16 = (f32[17]{0:T(128)S(1)}, f32[17]{0:T(128)}, u32[]{:S(2)}) copy-start(f32[17]{0:T(128)} %and_convert_fusion) | copy-start | bytes 208
  126.3 18.8 %all-to-all-start.2 = ((f32[10,32,128]{2,0,1:T(8,128)}), f32[10,32,128]{2,0,1:T(8,128)}, u32[]{:S(2)}, u32[]{:S(2)}) async-start(f32[10,32,128]{2,0,1:T(8,128)} %copy.843), calls=%async_computation.3 | async-start | bytes 524288 | tf_op jit(solution)/shard_map/all_to_all | solution.py:162
  137.5 13.8 %copy-start.7 = (f32[3,17,16,256]{3,2,1,0:T(8,128)S(1)}, f32[3,17,16,256]{3,2,1,0:T(8,128)}, u32[]{:S(2)}) copy-start(f32[3,17,16,256]{3,2,1,0:T(8,128)} %get-tuple-element.55) | copy-start | bytes 2506756
  145.1 14.7 %all-to-all-start = ((f32[32,1,1280]{2,1,0:T(1,128)}), f32[32,1,1280]{2,1,0:T(1,128)S(1)}, u32[]{:S(2)}, u32[]{:S(2)}) async-start(f32[32,1,1280]{2,1,0:T(1,128)} %reshape.211), calls=%async_computation.1 | async-start | bytes 327680 | tf_op jit(solution)/shard_map/all_to_all | solution.py:52
  165.4 5.1 %copy-start.10 = (f32[5,16,16,1]{2,0,1,3:T(8,128)S(1)}, f32[5,16,16,1]{2,0,1,3:T(8,128)}, u32[]{:S(2)}) copy-start(f32[5,16,16,1]{2,0,1,3:T(8,128)} %copy-done.9) | copy-start | bytes 15364
  165.4 5.1 %copy-start.15 = (pred[16]{0:T(512)(128)(4,1)S(1)}, pred[16]{0:T(512)(128)(4,1)}, u32[]{:S(2)}) copy-start(pred[16]{0:T(512)(128)(4,1)} %compare_and_fusion.2) | copy-start | bytes 52
  174.4 1.2 copy-start.3
  174.5 1.5 copy-start.5
  181.3 9.9 %collective-permute-start.9 = (f32[5,16,16]{2,0,1:T(8,128)S(1)}, f32[5,16,16]{2,0,1:T(8,128)S(1)}, u32[]{:S(2)}, u32[]{:S(2)}) collective-permute-start(f32[5,16,16]{2,0,1:T(8,128)S(1)} %bitcast_select_fusion.2), channel_id=1, source_target_pairs={{0,1},{1,0},{2,3},{3,2},{4,5},{5,4},{6,7},{7,6},{8,9},{9,8},{10,11... | collective-permute-start | bytes 15368 | tf_op jit(solution)/shard_map/ppermute | solution.py:19
  183.3 18.7 %collective-permute-start.5 = (f32[4,1,16,256]{3,2,1,0:T(8,128)S(1)}, f32[4,1,16,256]{3,2,1,0:T(8,128)S(1)}, u32[]{:S(2)}, u32[]{:S(2)}) collective-permute-start(f32[4,1,16,256]{3,2,1,0:T(8,128)S(1)} %get-tuple-element.53), channel_id=1, source_target_pairs={{0,16},{16,32},{32,48},{48,64},{64,80},{80,96},{96,112},{112,128},... | collective-permute-start | bytes 196616 | tf_op jit(solution)/shard_map/ppermute | solution.py:29
  186.7 15.3 %collective-permute-start.6 = (f32[4,1,16,256]{3,2,1,0:T(8,128)S(1)}, f32[4,1,16,256]{3,2,1,0:T(8,128)S(1)}, u32[]{:S(2)}, u32[]{:S(2)}) collective-permute-start(f32[4,1,16,256]{3,2,1,0:T(8,128)S(1)} %get-tuple-element.54), channel_id=1, source_target_pairs={{16,0},{32,16},{48,32},{64,48},{80,64},{96,80},{112,96},{128,112},... | collective-permute-start | bytes 196616 | tf_op jit(solution)/shard_map/ppermute | solution.py:31
  195.0 20.1 %all-to-all-start.1 = ((f32[32,1,1280]{2,1,0:T(1,128)}), f32[32,1,1280]{2,1,0:T(1,128)S(1)}, u32[]{:S(2)}, u32[]{:S(2)}) async-start(f32[32,1,1280]{2,1,0:T(1,128)} %reshape.213), calls=%async_computation.2 | async-start | bytes 327680 | tf_op jit(solution)/shard_map/all_to_all | solution.py:52
  202.4 9.2 %collective-permute-start.7 = (f32[4,18,1,256]{3,0,2,1:T(4,128)S(1)}, f32[4,18,1,256]{3,0,2,1:T(4,128)S(1)}, u32[]{:S(2)}, u32[]{:S(2)}) collective-permute-start(f32[4,18,1,256]{3,0,2,1:T(4,128)S(1)} %copy.875), channel_id=1, source_target_pairs={{0,2},{2,4},{4,6},{6,8},{8,10},{10,12},{12,14},{14,0},{1,3},{3,5},... | collective-permute-start | bytes 221192 | tf_op jit(solution)/shard_map/ppermute | solution.py:29
  207.2 7.5 %collective-permute-start.8 = (f32[4,18,1,256]{3,0,2,1:T(4,128)S(1)}, f32[4,18,1,256]{3,0,2,1:T(4,128)S(1)}, u32[]{:S(2)}, u32[]{:S(2)}) collective-permute-start(f32[4,18,1,256]{3,0,2,1:T(4,128)S(1)} %copy.876), channel_id=1, source_target_pairs={{2,0},{4,2},{6,4},{8,6},{10,8},{12,10},{14,12},{0,14},{3,1},{5,3},... | collective-permute-start | bytes 221192 | tf_op jit(solution)/shard_map/ppermute | solution.py:31
  229.1 1.3 copy-start.4
  230.4 1.8 copy-start.1
Sparse Core Ops, SparseCore 0:
  24.7 37.1 reduce-scatter.1
